TPU v7x, 32 devices: a whole 2x2x4 slice. The times are simulated.
32 devices in a mesh: section: 4 (over y, core), seq: 4 (over z), tp: 2 (over x).
Axes of the slice: x: 2, y: 2, z: 4, core: 2. Of those that a mesh axis runs over, the one named last changes fastest.
Arguments:
- queries: bfloat16 [768, 4096], P('seq', 'tp'), may hold values from -45 to 45
- keys: bfloat16 [64, 4096], P(('section', 'seq'), 'tp'), may hold values from -6 to 6
- values: bfloat16 [64, 4096], P(('section', 'seq'), 'tp'), may hold values from -6 to 6
- out_grad: bfloat16 [768, 4096], P('seq', 'tp'), may hold values from -48 to 48
- text_len: int32 [2], replicated, may hold values from 192 to 384, as said below
- key_len: int32 [4], replicated, may hold values from 8 to 16, as said below
Outputs:
- query_grad: bfloat16 [768, 4096], P('seq', 'tp')
- key_grad: float32 [64, 4096], P(('section', 'seq'), 'tp')
- value_grad: float32 [64, 4096], P(('section', 'seq'), 'tp')
Inputs may be any that keep to these rules, and one draw needn't show every extreme that they name: `text_len`: one length per report sequence of 384 rows; rows at or past it are padding. `key_len`: live volume tokens of each slab of 16; the slab's later tokens are padding.
All inputs are finite; a program needn't handle non-finite values.
Results may differ from a plain program's by a relative error of at most 0.009.
Values may be sent and summed in bfloat16 or wider, within the bound.
A program may use at most 64 MiB of HBM per device.

v0:
```python
import math
import jax
import jax.numpy as jnp
from jax import lax
from jax.sharding import PartitionSpec as P

HD = 128
SEQS = 2


def joined(x, axis, combine):
    everything = jax.tree.map(lambda part: lax.all_gather(part, axis), x)
    initial = jax.tree.map(lambda part: part[0], everything)

    def hop(k, so_far):
        return combine(so_far, jax.tree.map(lambda part: part[k], everything))

    return lax.fori_loop(1, lax.axis_size(axis), hop, initial)


def combine_full(left_part, right_part):
    top = jnp.maximum(left_part[0], right_part[0])
    left_factor = jnp.exp(left_part[0] - top)
    right_factor = jnp.exp(right_part[0] - top)
    total = left_part[1] * left_factor + right_part[1] * right_factor
    merged = left_part[2] * left_factor[..., None] + right_part[2] * right_factor[..., None]
    return (top, total, merged)


def per_device(queries, keys, values, out_grad, text_len, key_len):
    score_scale = 1.0 / math.sqrt(HD)
    row_count = queries.shape[0]
    feat_width = queries.shape[1]
    head_count = feat_width // HD
    length_rows = row_count * lax.axis_size("seq") // SEQS
    position = lax.axis_index("seq") * row_count + jnp.arange(row_count, dtype=jnp.int32)
    seq_ids = position // length_rows
    limits = jnp.sum(
        jnp.where(
            seq_ids[:, None] == jnp.arange(SEQS, dtype=jnp.int32)[None, :], text_len[None, :], 0
        ),
        axis=1,
    )
    masked_grad = jnp.where(
        (position % length_rows < limits)[:, None], out_grad, jnp.zeros_like(out_grad)
    )
    slab_index = lax.axis_index("section")
    live_count = jnp.sum(
        jnp.where(jnp.arange(key_len.shape[0], dtype=jnp.int32) == slab_index, key_len, 0)
    )
    key_all, value_all = (
        lax.all_gather(keys, "seq", axis=0, tiled=True),
        lax.all_gather(values, "seq", axis=0, tiled=True),
    )
    key_total = key_all.shape[0]
    query_heads = queries.reshape(row_count, head_count, HD)
    grad_heads = masked_grad.reshape(row_count, head_count, HD)
    key_heads = key_all.reshape(key_total, head_count, HD)
    value_heads = value_all.reshape(key_total, head_count, HD)
    scores = (
        jnp.einsum("qhd,khd->qhk", query_heads, key_heads, preferred_element_type=jnp.float32)
        * score_scale
    )
    key_live = jnp.arange(key_total, dtype=jnp.int32) < live_count
    scores = jnp.where(key_live[None, None, :], scores, jnp.float32(-1e30))
    local_max = jnp.max(scores, axis=-1)
    expo = jnp.exp(scores - local_max[..., None])
    local_total = jnp.sum(expo, axis=-1)
    weighted = jnp.einsum(
        "qhk,khd->qhd", expo.astype(jnp.bfloat16), value_heads, preferred_element_type=jnp.float32
    )
    row_max, total, merged = joined((local_max, local_total, weighted), "section", combine_full)
    row_dot = jnp.sum(grad_heads * (merged / total[..., None]), axis=-1)
    probs = jnp.exp(scores - row_max[..., None]) / total[..., None]
    probs_low = probs.astype(jnp.bfloat16)
    prob_grad = jnp.einsum(
        "qhd,khd->qhk", grad_heads, value_heads, preferred_element_type=jnp.float32
    )
    score_grad = (probs * (prob_grad - row_dot[..., None])).astype(jnp.bfloat16)
    query_share = (
        jnp.einsum("qhk,khd->qhd", score_grad, key_heads, preferred_element_type=jnp.float32)
        * score_scale
    )
    query_grad = lax.psum(
        query_share.reshape(row_count, feat_width).astype(jnp.bfloat16), "section"
    )
    term_rows = lax.axis_size("seq") * keys.shape[0]
    key_term = (
        jnp.einsum("qhk,qhd->khd", score_grad, query_heads, preferred_element_type=jnp.float32)
        * score_scale
    )
    value_term = jnp.einsum(
        "qhk,qhd->khd", probs_low, grad_heads, preferred_element_type=jnp.float32
    )
    summed = lax.psum_scatter(
        jnp.stack(
            [key_term.reshape(term_rows, feat_width), value_term.reshape(term_rows, feat_width)],
            axis=1,
        ),
        "seq",
        scatter_dimension=0,
        tiled=True,
    )
    return (query_grad, summed[:, 0], summed[:, 1])


def solution(mesh):
    in_specs = (
        P("seq", "tp"),
        P(("section", "seq"), "tp"),
        P(("section", "seq"), "tp"),
        P("seq", "tp"),
        P(),
        P(),
    )
    out_specs = (P("seq", "tp"), P(("section", "seq"), "tp"), P(("section", "seq"), "tp"))
    return jax.shard_map(
        per_device, mesh=mesh, in_specs=in_specs, out_specs=out_specs, check_vma=False
    )
```

profile of v0, /device:TPU:0, one launch (start us, length us, event | category | flops | bytes accessed | tf_op | source)
XLA Modules:
  0.0 193.0 jit_solution(14795662915115848886)
XLA Ops:
  7.2 15.3 %all-gather.3 = bf16[4,4,2048]{2,1,0:T(4,128)(2,1)S(1)} all-gather(bf16[1,4,2048]{2,1,0:T(4,128)(2,1)} %bitcast.88), channel_id=1, replica_groups=mesh['section'=4,'seq'=4,'tp'=2] {'seq'}, dimensions={0}, use_global_device_ids=true | all-gather | bytes 81920 | tf_op jit(solution)/shard_map/all_gather | solution.py:52
  22.6 1.3 fusion.34
  24.5 13.5 %all-gather.6 = bf16[4,4,2048]{2,1,0:T(4,128)(2,1)S(1)} all-gather(bf16[1,4,2048]{2,1,0:T(4,128)(2,1)} %bitcast.89), channel_id=1, replica_groups=mesh['section'=4,'seq'=4,'tp'=2] {'seq'}, dimensions={0}, use_global_device_ids=true | all-gather | bytes 81920 | tf_op jit(solution)/shard_map/all_gather | solution.py:53
  38.7 1.6 convolution_bitcast_fusion
  40.5 1.1 fusion.20
  41.8 5.2 %all-gather.5 = f32[4,192,16]{1,2,0:T(8,128)S(1)} all-gather(f32[1,192,16]{1,2,0:T(8,128)S(1)} %bitcast.87), channel_id=3, replica_groups=mesh['section'=4,'seq'=4,'tp'=2] {'section'}, dimensions={0}, use_global_device_ids=true | all-gather | bytes 61440 | tf_op jit(solution)/shard_map/all_gather | solution.py:12
  47.1 5.7 %all-gather.4 = f32[4,192,16]{1,2,0:T(8,128)} all-gather(f32[1,192,16]{1,2,0:T(8,128)S(1)} %bitcast.86), channel_id=2, replica_groups=mesh['section'=4,'seq'=4,'tp'=2] {'section'}, dimensions={0}, use_global_device_ids=true | all-gather | bytes 61440 | tf_op jit(solution)/shard_map/all_gather | solution.py:12
  53.4 34.3 %all-gather.9.cloned.1.call-done = f32[768,16,128]{2,0,1:T(8,128)} async-done(((f32[192,16,128]{2,0,1:T(8,128)}), f32[768,16,128]{2,0,1:T(8,128)}) %all-gather.9.cloned.1.call-update) | async-done | bytes 6291472 | tf_op jit(solution)/shard_map/all_gather | solution.py:12
  87.8 1.4 slice-done
  90.1 14.3 %while.19 = (s32[]{:T(128)}, f32[192,16]{0,1:T(8,128)S(1)}, f32[192,16]{0,1:T(8,128)S(1)}, f32[192,16,128]{2,1,0:T(8,128)S(1)}, f32[4,192,16]{1,2,0:T(8,128)}, /...) while((s32[]{:T(128)}, f32[192,16]{0,1:T(8,128)S(1)}, ...), condition=%wide.region_4.5_spmd, body=%wide.region_3.4_spmd.sunk | while | flops 1198085 | bytes 8036503 | solution.py:18
  91.0 1.5 constant_dynamic-slice_fusion.2
  92.6 2.3 %fusion.44 = f32[192,16,128]{2,1,0:T(8,128)S(1)} fusion(f32[1,192,16,128]{3,1,0,2:T(8,128)S(1)} %constant_dynamic-slice_fusion.2, f32[192,16,128]{2,1,0:T(8,128)S(1)} %get-tuple-element.300, f32[192,16]{1,0:T(8,128)S(1)} %copy.114, f32[192,16]{1,0:T(8,128)S(1)} %copy.115), kind=kLoop, calls=%fused_computation.2.clone.1 | loop fusion | flops 1179648 | bytes 4743168 | tf_op jit(solution)/shard_map/while/body/eval_jaxpr/add | solution.py:26
  95.8 1.5 constant_dynamic-slice_fusion.2
  97.4 2.3 %fusion.44 = f32[192,16,128]{2,1,0:T(8,128)S(1)} fusion(f32[1,192,16,128]{3,1,0,2:T(8,128)S(1)} %constant_dynamic-slice_fusion.2, f32[192,16,128]{2,1,0:T(8,128)S(1)} %get-tuple-element.300, f32[192,16]{1,0:T(8,128)S(1)} %copy.114, f32[192,16]{1,0:T(8,128)S(1)} %copy.115), kind=kLoop, calls=%fused_computation.2.clone.1 | loop fusion | flops 1179648 | bytes 4743168 | tf_op jit(solution)/shard_map/while/body/eval_jaxpr/add | solution.py:26
  100.6 1.5 constant_dynamic-slice_fusion.2
  102.1 2.3 %fusion.44 = f32[192,16,128]{2,1,0:T(8,128)S(1)} fusion(f32[1,192,16,128]{3,1,0,2:T(8,128)S(1)} %constant_dynamic-slice_fusion.2, f32[192,16,128]{2,1,0:T(8,128)S(1)} %get-tuple-element.300, f32[192,16]{1,0:T(8,128)S(1)} %copy.114, f32[192,16]{1,0:T(8,128)S(1)} %copy.115), kind=kLoop, calls=%fused_computation.2.clone.1 | loop fusion | flops 1179648 | bytes 4743168 | tf_op jit(solution)/shard_map/while/body/eval_jaxpr/add | solution.py:26
  104.5 1.5 convolution_bitcast_fusion.2
  106.8 0.9 multiply_reduce_fusion
  107.8 1.8 fusion.9
  111.2 1.1 copy.109
  113.5 32.9 %all-reduce.6.cloned.1.call-done = f32[16,2,2048]{2,0,1:T(8,128)} async-done(((f32[16,2,2048]{2,0,1:T(8,128)}), f32[16,2,2048]{2,0,1:T(8,128)}) %all-reduce.6.cloned.1.call-update) | async-done | bytes 262160
  146.5 1.5 dynamic-slice_bitcast_fusion
  148.0 36.4 %all-reduce.4.cloned.1.call-done = bf16[192,2048]{1,0:T(8,128)(2,1)} async-done(((bf16[192,2048]{1,0:T(8,128)(2,1)}), bf16[192,2048]{1,0:T(8,128)(2,1)}) %all-reduce.4.cloned.1.call-update) | async-done | bytes 786448 | tf_op jit(solution)/shard_map/psum | solution.py:84
  184.4 2.1 %copy.130 = bf16[192,2048]{1,0:T(8,128)(2,1)} copy(bf16[192,2048]{1,0:T(8,128)(2,1)} %all-reduce.4.cloned.1.call-done) | data formatting | bytes 1572864
  (54 shorter events, 9.3 us)
Async XLA Ops:
  7.2 30.9 %copy-start = (bf16[192,2048]{1,0:T(8,128)(2,1)S(1)}, bf16[192,2048]{1,0:T(8,128)(2,1)}, u32[]{:S(2)}) copy-start(bf16[192,2048]{1,0:T(8,128)(2,1)} %param.8) | copy-start | bytes 2359300
  7.2 80.6 %all-gather.9.cloned.1.call-start = ((), (), s32[]{:S(2)}) async-start(), calls=%async_computation.1 | async-start | bytes 7864320 | tf_op jit(solution)/shard_map/all_gather | solution.py:12
  38.1 2.2 %copy-start.4 = (bf16[16,16,128]{2,1,0:T(8,128)(2,1)}, bf16[16,16,128]{2,1,0:T(8,128)(2,1)S(1)}, u32[]{:S(2)}) copy-start(bf16[16,16,128]{2,1,0:T(8,128)(2,1)S(1)} %reshape.54) | copy-start | bytes 196612
  38.7 3.1 %copy-start.1 = (f32[192,16,16]{0,2,1:T(8,128)}, f32[192,16,16]{0,2,1:T(8,128)S(1)}, u32[]{:S(2)}) copy-start(f32[192,16,16]{0,2,1:T(8,128)S(1)} %get-tuple-element.235) | copy-start | bytes 589828
  38.7 1.7 copy-start.6
  38.7 1.8 copy-start.2
  40.3 106.2 %all-reduce.6.cloned.1.call-start = ((), (), s32[]{:S(2)}) async-start(), calls=%async_computation.2 | async-start | bytes 524288
  87.8 1.4 slice-start
  106.0 1.7 copy-start.5
  107.8 2.2 %copy-start.3 = (f32[16,1,2048]{2,0,1:T(8,128)S(1)}, f32[16,1,2048]{2,0,1:T(8,128)}, u32[]{:S(2)}) copy-start(f32[16,1,2048]{2,0,1:T(8,128)} %stack_reshape.7) | copy-start | bytes 393220
  110.7 1.6 copy-start.7
  110.7 73.7 %all-reduce.4.cloned.1.call-start = ((), (), s32[]{:S(2)}) async-start(), calls=%async_computation | async-start | bytes 1572864 | tf_op jit(solution)/shard_map/psum | solution.py:84
Sparse Core Ops, SparseCore 0:
  40.4 47.2 all-gather.8
  110.8 35.6 all-reduce.5
  149.4 34.8 all-reduce.3
where the time goes:
time: 194 us; the launch traced here: 193 us
  waiting for transfers between devices  104 us (54%)
  blocking collectives  39.7 us (20%)
  local copies, waits for them, and re-layouts  14.8 us (8%)
  between operations  14.6 us (8%)
  other arithmetic  13.8 us (7%)
  matrix products  6.16 us (3%)
    psum x1, waiting for transfers between devices, per_device(): lax.psum(query_share.reshape(row_count, feat_width).astype(jnp.bfloat16),...  36.4 us
    all_gather x1, waiting for transfers between devices, joined(): everything = jax.tree.map(lambda part: lax.all_gather(part, axis), x)  34.3 us
    unnamed x4, waiting for transfers between devices  33 us
    all_gather x1, blocking collectives, per_device(): lax.all_gather(keys, 'seq', axis=0, tiled=True)  15.3 us
    all_gather x1, blocking collectives, per_device(): lax.all_gather(values, 'seq', axis=0, tiled=True)  13.5 us
    all_gather x2, blocking collectives, joined(): everything = jax.tree.map(lambda part: lax.all_gather(part, axis), x)  10.9 us
    add x3, other arithmetic, combine_full(): left_part[2] * left_factor[..., None]  6.79 us
    dynamic_slice x3, local copies, waits for them, and re-layouts, hop(): return combine(so_far, jax.tree.map(lambda part: part[k], everything))  4.6 us
  transfers between devices with their start and end apart: 3, of which 3 were waited for; matrix products, arithmetic and copies ran while one was open for 3% of the time, Pallas kernels for 0%

commit v1 on v0

--- a/solution.py
+++ b/solution.py
@@ -81,9 +81,8 @@
         jnp.einsum("qhk,khd->qhd", score_grad, key_heads, preferred_element_type=jnp.float32)
         * score_scale
     )
-    query_grad = lax.psum(
-        query_share.reshape(row_count, feat_width).astype(jnp.bfloat16), "section"
-    )
+    t0 = query_share.reshape(row_count, feat_width).astype(jnp.bfloat16)
+    query_grad = lax.all_gather(t0, axis_name="section").sum(axis=0)
     term_rows = lax.axis_size("seq") * keys.shape[0]
     key_term = (
         jnp.einsum("qhk,qhd->khd", score_grad, query_heads, preferred_element_type=jnp.float32)

time: 194 us -> 188 us (0.969)
  waiting for transfers between devices: 104 us -> 95.7 us
  other arithmetic: 13.8 us -> 17.4 us
    psum x1 -> x0, waiting for transfers between devices: 36.4 us -> none  [per_device(): lax.psum(query_share.reshape(row_count, feat_width).astype(jnp.bfloat16),...]
    all_gather x0 -> x1, waiting for transfers between devices: none -> 29 us  [per_device(): query_grad = lax.all_gather(t0, axis_name='section').sum(axis=0)]
    reduce_sum x0 -> x1, other arithmetic: none -> 3.59 us  [per_device(): query_grad = lax.all_gather(t0, axis_name='section').sum(axis=0)]
    unnamed x19 -> x18, local copies, waits for them, and re-layouts: 2.88 us -> 0.79 us
where the time goes in v1:
time: 188 us; the launch traced here: 187 us
  waiting for transfers between devices  95.7 us (51%)
  blocking collectives  39.7 us (21%)
  other arithmetic  17.4 us (9%)
  between operations  14.6 us (8%)
  local copies, waits for them, and re-layouts  13.3 us (7%)
  matrix products  6.16 us (3%)
    all_gather x1, waiting for transfers between devices, joined(): everything = jax.tree.map(lambda part: lax.all_gather(part, axis), x)  34.3 us
    unnamed x4, waiting for transfers between devices  32.3 us
    all_gather x1, waiting for transfers between devices, per_device(): query_grad = lax.all_gather(t0, axis_name='section').sum(axis=0)  29 us
    all_gather x1, blocking collectives, per_device(): lax.all_gather(keys, 'seq', axis=0, tiled=True)  15.3 us
    all_gather x1, blocking collectives, per_device(): lax.all_gather(values, 'seq', axis=0, tiled=True)  13.5 us
    all_gather x2, blocking collectives, joined(): everything = jax.tree.map(lambda part: lax.all_gather(part, axis), x)  10.9 us
    add x3, other arithmetic, combine_full(): left_part[2] * left_factor[..., None]  6.79 us
    dynamic_slice x3, local copies, waits for them, and re-layouts, hop(): return combine(so_far, jax.tree.map(lambda part: part[k], everything))  4.6 us
  transfers between devices with their start and end apart: 3, of which 3 were waited for; matrix products, arithmetic and copies ran while one was open for 3% of the time, Pallas kernels for 0%

profile of v1, /device:TPU:0, one launch (start us, length us, event | category | flops | bytes accessed | tf_op | source)
XLA Modules:
  0.0 187.2 jit_solution(14585013394853931367)
XLA Ops:
  7.2 15.3 %all-gather.3 = bf16[4,4,2048]{2,1,0:T(4,128)(2,1)S(1)} all-gather(bf16[1,4,2048]{2,1,0:T(4,128)(2,1)} %bitcast.83), channel_id=1, replica_groups=mesh['section'=4,'seq'=4,'tp'=2] {'seq'}, dimensions={0}, use_global_device_ids=true | all-gather | bytes 81920 | tf_op jit(solution)/shard_map/all_gather | solution.py:52
  22.6 1.3 fusion.34
  24.5 13.5 %all-gather.6 = bf16[4,4,2048]{2,1,0:T(4,128)(2,1)S(1)} all-gather(bf16[1,4,2048]{2,1,0:T(4,128)(2,1)} %bitcast.84), channel_id=1, replica_groups=mesh['section'=4,'seq'=4,'tp'=2] {'seq'}, dimensions={0}, use_global_device_ids=true | all-gather | bytes 81920 | tf_op jit(solution)/shard_map/all_gather | solution.py:53
  38.7 1.6 convolution_bitcast_fusion
  40.5 1.1 fusion.20
  41.8 5.2 %all-gather.5 = f32[4,192,16]{1,2,0:T(8,128)S(1)} all-gather(f32[1,192,16]{1,2,0:T(8,128)S(1)} %bitcast.82), channel_id=3, replica_groups=mesh['section'=4,'seq'=4,'tp'=2] {'section'}, dimensions={0}, use_global_device_ids=true | all-gather | bytes 61440 | tf_op jit(solution)/shard_map/all_gather | solution.py:12
  47.1 5.7 %all-gather.4 = f32[4,192,16]{1,2,0:T(8,128)} all-gather(f32[1,192,16]{1,2,0:T(8,128)S(1)} %bitcast.81), channel_id=2, replica_groups=mesh['section'=4,'seq'=4,'tp'=2] {'section'}, dimensions={0}, use_global_device_ids=true | all-gather | bytes 61440 | tf_op jit(solution)/shard_map/all_gather | solution.py:12
  53.4 34.3 %all-gather.12.cloned.1.call-done = f32[768,16,128]{2,0,1:T(8,128)} async-done(((f32[192,16,128]{2,0,1:T(8,128)}), f32[768,16,128]{2,0,1:T(8,128)}) %all-gather.12.cloned.1.call-update) | async-done | bytes 6291472 | tf_op jit(solution)/shard_map/all_gather | solution.py:12
  87.8 1.4 slice-done
  90.1 14.3 %while.19 = (s32[]{:T(128)}, f32[192,16]{0,1:T(8,128)S(1)}, f32[192,16]{0,1:T(8,128)S(1)}, f32[192,16,128]{2,1,0:T(8,128)S(1)}, f32[4,192,16]{1,2,0:T(8,128)}, /...) while((s32[]{:T(128)}, f32[192,16]{0,1:T(8,128)S(1)}, ...), condition=%wide.region_4.5_spmd, body=%wide.region_3.4_spmd.sunk | while | flops 1198085 | bytes 8036503 | solution.py:18
  91.0 1.5 constant_dynamic-slice_fusion.2
  92.6 2.3 %fusion.44 = f32[192,16,128]{2,1,0:T(8,128)S(1)} fusion(f32[1,192,16,128]{3,1,0,2:T(8,128)S(1)} %constant_dynamic-slice_fusion.2, f32[192,16,128]{2,1,0:T(8,128)S(1)} %get-tuple-element.300, f32[192,16]{1,0:T(8,128)S(1)} %copy.111, f32[192,16]{1,0:T(8,128)S(1)} %copy.112), kind=kLoop, calls=%fused_computation.2.clone.1 | loop fusion | flops 1179648 | bytes 4743168 | tf_op jit(solution)/shard_map/while/body/eval_jaxpr/add | solution.py:26
  95.8 1.5 constant_dynamic-slice_fusion.2
  97.4 2.3 %fusion.44 = f32[192,16,128]{2,1,0:T(8,128)S(1)} fusion(f32[1,192,16,128]{3,1,0,2:T(8,128)S(1)} %constant_dynamic-slice_fusion.2, f32[192,16,128]{2,1,0:T(8,128)S(1)} %get-tuple-element.300, f32[192,16]{1,0:T(8,128)S(1)} %copy.111, f32[192,16]{1,0:T(8,128)S(1)} %copy.112), kind=kLoop, calls=%fused_computation.2.clone.1 | loop fusion | flops 1179648 | bytes 4743168 | tf_op jit(solution)/shard_map/while/body/eval_jaxpr/add | solution.py:26
  100.6 1.5 constant_dynamic-slice_fusion.2
  102.1 2.3 %fusion.44 = f32[192,16,128]{2,1,0:T(8,128)S(1)} fusion(f32[1,192,16,128]{3,1,0,2:T(8,128)S(1)} %constant_dynamic-slice_fusion.2, f32[192,16,128]{2,1,0:T(8,128)S(1)} %get-tuple-element.300, f32[192,16]{1,0:T(8,128)S(1)} %copy.111, f32[192,16]{1,0:T(8,128)S(1)} %copy.112), kind=kLoop, calls=%fused_computation.2.clone.1 | loop fusion | flops 1179648 | bytes 4743168 | tf_op jit(solution)/shard_map/while/body/eval_jaxpr/add | solution.py:26
  104.5 1.5 convolution_bitcast_fusion.2
  106.8 0.9 multiply_reduce_fusion
  107.8 1.8 fusion.9
  111.7 1.2 convert_element_type.35
  114.2 32.3 %all-reduce.3.cloned.1.call-done = f32[16,2,2048]{2,0,1:T(8,128)} async-done(((f32[16,2,2048]{2,0,1:T(8,128)}), f32[16,2,2048]{2,0,1:T(8,128)}) %all-reduce.3.cloned.1.call-update) | async-done | bytes 262160
  146.5 1.5 dynamic-slice_bitcast_fusion
  148.0 29.0 %all-gather.10.cloned.1.call-done = bf16[4,192,2048]{2,1,0:T(8,128)(2,1)} async-done(((bf16[1,192,2048]{2,1,0:T(8,128)(2,1)}), bf16[4,192,2048]{2,1,0:T(8,128)(2,1)}) %all-gather.10.cloned.1.call-update) | async-done | bytes 3145744 | tf_op jit(solution)/shard_map/all_gather | solution.py:85
  177.0 3.6 %reduce_sum.52 = bf16[192,2048]{1,0:T(8,128)(2,1)} reduce(bf16[4,192,2048]{2,1,0:T(8,128)(2,1)} %all-gather.10.cloned.1.call-done, bf16[]{:T(256)} %constant.80.clone.1), dimensions={0}, to_apply=%region_7.8 | reduce | flops 1179648 | bytes 3932162 | tf_op jit(solution)/shard_map/reduce_sum | solution.py:85
  (55 shorter events, 9.8 us)
Async XLA Ops:
  7.2 30.9 %copy-start = (bf16[192,2048]{1,0:T(8,128)(2,1)S(1)}, bf16[192,2048]{1,0:T(8,128)(2,1)}, u32[]{:S(2)}) copy-start(bf16[192,2048]{1,0:T(8,128)(2,1)} %param.8) | copy-start | bytes 2359300
  7.2 80.6 %all-gather.12.cloned.1.call-start = ((), (), s32[]{:S(2)}) async-start(), calls=%async_computation.1 | async-start | bytes 7864320 | tf_op jit(solution)/shard_map/all_gather | solution.py:12
  38.1 2.2 %copy-start.4 = (bf16[16,16,128]{2,1,0:T(8,128)(2,1)}, bf16[16,16,128]{2,1,0:T(8,128)(2,1)S(1)}, u32[]{:S(2)}) copy-start(bf16[16,16,128]{2,1,0:T(8,128)(2,1)S(1)} %reshape.64) | copy-start | bytes 196612
  38.7 3.1 %copy-start.1 = (f32[192,16,16]{0,2,1:T(8,128)}, f32[192,16,16]{0,2,1:T(8,128)S(1)}, u32[]{:S(2)}) copy-start(f32[192,16,16]{0,2,1:T(8,128)S(1)} %get-tuple-element.235) | copy-start | bytes 589828
  38.7 1.7 copy-start.6
  38.7 1.8 copy-start.2
  40.3 106.2 %all-reduce.3.cloned.1.call-start = ((), (), s32[]{:S(2)}) async-start(), calls=%async_computation.2 | async-start | bytes 524288
  87.8 1.4 slice-start
  106.0 1.7 copy-start.5
  107.8 2.2 %copy-start.3 = (f32[16,1,2048]{2,0,1:T(8,128)S(1)}, f32[16,1,2048]{2,0,1:T(8,128)}, u32[]{:S(2)}) copy-start(f32[16,1,2048]{2,0,1:T(8,128)} %stack_reshape.7) | copy-start | bytes 393220
  110.7 66.4 %all-gather.10.cloned.1.call-start = ((), (), s32[]{:S(2)}) async-start(), calls=%async_computation | async-start | bytes 3932160 | tf_op jit(solution)/shard_map/all_gather | solution.py:85
  111.7 1.3 copy-start.7
Sparse Core Ops, SparseCore 0:
  40.4 47.2 all-gather.11
  110.8 35.6 all-reduce.2
  148.6 28.3 all-gather.9
